TPU v7x, 256 devices: a whole 4x4x8 slice. The times are simulated.
256 devices in a mesh: row: 8 (over y, z_hi), col: 32 (over z_lo, x, core).
Axes of the slice: x: 4, y: 4, z: 8 (z_hi: 2, z_lo: 4; z = z_hi * 4 + z_lo), core: 2. Of those that a mesh axis runs over, the one named last changes fastest.
Arguments:
- embedding: bfloat16 [98304, 256], P(('col', 'row')), may hold values from -6 to 6
- weight: bfloat16 [256, 256], replicated, may hold values from -0.375 to 0.375
- grad_out: bfloat16 [98304, 256], P(('row', 'col')), may hold values from -6 to 6
- in_degree: int32 [98304], P(('row', 'col')), may hold values from 4 to 64
- out_degree: int32 [98304], P(('col', 'row')), may hold values from 4 to 64
- tile_edges: bfloat16 [8, 32, 192, 128, 128], P('row', 'col'), may hold values from 0 to 2, as said below
- tile_coords: int32 [8, 32, 192, 2], P('row', 'col'), may hold values from 0 to 95, as said below
- tile_count: int32 [8, 32], P('row', 'col'), may hold values from 48 to 192, as said below
Outputs:
- hidden: bfloat16 [98304, 256], P(('row', 'col'))
- grad_embedding: float32 [98304, 256], P(('col', 'row'))
- grad_weight: float32 [256, 256], replicated
Inputs may be any that keep to these rules, and one draw needn't show every extreme that they name: `tile_coords`: slots of one block name distinct tiles; entry 0 is a tile row below 96, entry 1 a tile column below 24. The live slots of a block are its first tile_count slots; some block has all 192 slots live. `tile_edges`: each entry is zero or a positive edge weight.
All inputs are finite; a program needn't handle non-finite values.
Results may differ from a plain program's by a relative error of at most 0.033.
Values may be sent and summed in bfloat16 or wider, within the bound.
No kernel may reach another device: no remote copies, remote signals or barrier semaphores. Data moves between devices by JAX's collectives and lax.ppermute only.
A program may use at most 128 MiB of HBM per device.

v0:
```python
import math

import jax
import jax.numpy as jnp
from jax import lax
from jax.sharding import PartitionSpec as P

decay_rate = 0.01


def tile_products(tile_set, source_ids, target_ids, alive, lookup, out_count, flipped):
    slots = tile_set.shape[0]
    block_count = max(1, slots // 64)
    per_block = slots // block_count

    def advance(running, number):
        first_slot = number * per_block
        block_tiles = lax.dynamic_slice_in_dim(tile_set, first_slot, per_block, 0)
        chosen = lax.dynamic_slice_in_dim(source_ids, first_slot, per_block, 0)
        picked = jnp.take(lookup, chosen, axis=0)
        if flipped:
            products = jnp.einsum(
                "tij,tif->tjf", block_tiles, picked, preferred_element_type=jnp.float32
            )
        else:
            products = jnp.einsum(
                "tij,tjf->tif", block_tiles, picked, preferred_element_type=jnp.float32
            )
        targets = lax.dynamic_slice_in_dim(target_ids, first_slot, per_block, 0)
        weights_alive = lax.dynamic_slice_in_dim(alive, first_slot, per_block, 0)
        products = products * weights_alive[:, None, None]
        running = running + jax.ops.segment_sum(products, targets, num_segments=out_count)
        return (running, None)

    initial = jnp.zeros((out_count, lookup.shape[1], lookup.shape[2]), jnp.float32)
    result, _ = lax.scan(advance, initial, jnp.arange(block_count))
    return result


def per_device(
    embedding, weight, grad_out, in_degree, out_degree, tile_edges, tile_coords, tile_count
):
    tile_set = tile_edges[0, 0]
    coords = tile_coords[0, 0]
    live_count = tile_count[0, 0]
    n_row = lax.axis_size("row")
    n_col = lax.axis_size("col")
    own_rows, width = embedding.shape
    edge_size = tile_set.shape[1]
    block_rows = own_rows * n_col
    block_cols = own_rows * n_row
    tile_rows = block_rows // edge_size
    tile_cols = block_cols // edge_size
    total_nodes = own_rows * n_row * n_col
    alive = (jnp.arange(tile_set.shape[0]) < live_count).astype(jnp.float32)
    scale_out = lax.rsqrt(out_degree.astype(jnp.float32))
    scaled = (scale_out[:, None] * embedding.astype(jnp.float32)).astype(jnp.bfloat16)
    source_block = lax.all_gather(scaled, "row", axis=0, tiled=True)
    forward_terms = tile_products(
        tile_set,
        coords[:, 1],
        coords[:, 0],
        alive,
        source_block.reshape(tile_cols, edge_size, width),
        tile_rows,
        False,
    )
    forward_terms = forward_terms.reshape(block_rows, width)
    summed = lax.psum_scatter(
        forward_terms.astype(jnp.bfloat16), "col", scatter_dimension=0, tiled=True
    ).astype(jnp.float32)
    scale_in = lax.rsqrt(in_degree.astype(jnp.float32))
    aggregate = (scale_in[:, None] * summed).astype(jnp.bfloat16)
    preact = jnp.dot(aggregate, weight, preferred_element_type=jnp.float32)
    gates = jax.nn.sigmoid(preact)
    hidden = (preact * gates).astype(jnp.bfloat16)
    delta_rows = (grad_out.astype(jnp.float32) * gates * (1.0 + preact * (1.0 - gates))).astype(
        jnp.bfloat16
    )
    local_weight = lax.dot_general(
        aggregate, delta_rows, (((0,), (0,)), ((), ())), preferred_element_type=jnp.float32
    )
    grad_weight = lax.psum(local_weight, ("row", "col")) / math.sqrt(total_nodes)
    projected = lax.dot_general(
        delta_rows, weight, (((1,), (1,)), ((), ())), preferred_element_type=jnp.float32
    )
    upstream = (scale_in[:, None] * projected).astype(jnp.bfloat16)
    upstream_block = lax.all_gather(upstream, "col", axis=0, tiled=True)
    backward_terms = tile_products(
        tile_set,
        coords[:, 0],
        coords[:, 1],
        alive,
        upstream_block.reshape(tile_rows, edge_size, width),
        tile_cols,
        True,
    )
    backward_terms = backward_terms.reshape(block_cols, width)
    source_total = lax.psum_scatter(
        backward_terms.astype(jnp.bfloat16), "row", scatter_dimension=0, tiled=True
    ).astype(jnp.float32)
    decay = decay_rate * jnp.sqrt(out_degree.astype(jnp.float32))
    grad_embedding = scale_out[:, None] * source_total + decay[:, None] * embedding.astype(
        jnp.float32
    )
    return (hidden, grad_embedding, grad_weight)


def solution(mesh):
    in_specs = (
        P(("col", "row"), None),
        P(),
        P(("row", "col"), None),
        P(("row", "col")),
        P(("col", "row")),
        P("row", "col", None, None, None),
        P("row", "col", None, None),
        P("row", "col"),
    )
    out_specs = (P(("row", "col"), None), P(("col", "row"), None), P())
    return jax.shard_map(
        per_device, mesh=mesh, in_specs=in_specs, out_specs=out_specs, check_vma=False
    )
```

profile of v0, /device:TPU:2, one launch (start us, length us, event | category | flops | bytes accessed | tf_op | source)
XLA Modules:
  0.0 763.6 jit_solution(9937921684894183327)
XLA Ops:
  9.1 1.7 fusion.19
  12.3 71.1 %all-gather.3.cloned.1.call-done = bf16[3072,256]{1,0:T(8,128)(2,1)} async-done(((bf16[384,256]{1,0:T(8,128)(2,1)}), bf16[3072,256]{1,0:T(8,128)(2,1)}) %all-gather.3.cloned.1.call-update) | async-done | bytes 1572880 | tf_op jit(solution)/shard_map/all_gather | solution.py:58
  83.4 6.1 broadcast.23
  89.5 93.9 %while.20 = (s32[]{:T(128)}, f32[96,128,256]{2,1,0:T(8,128)}, s32[3]{0:T(128)S(1)}, s32[192]{0:T(256)S(1)}, bf16[192,128,128]{2,1,0:T(8,128)(2,1)}, /*index=5*/s...) while((s32[]{:T(128)}, f32[96,128,256]{2,1,0:T(8,128)}, ...), condition=%wide.region_2.3_spmd, body=%wide.region_0.2_spmd.sunk | while | flops 543163776 | bytes 48241472 | solution.py:36
  90.8 2.8 gather_fusion
  93.7 7.4 broadcast_multiply_fusion.5
  101.1 19.8 %scatter_fusion = f32[96,128,256]{2,1,0:T(8,128)} fusion(f32[96,128,256]{2,1,0:T(8,128)} %get-tuple-element.258, s32[64]{0:T(128)S(1)} %dynamic_slice.49, f32[64,128,256]{2,1,0:T(8,128)} %broadcast_multiply_fusion.5), kind=kCustom, calls=%fused_computation.2.clone.1 | custom fusion | flops 2097152 | bytes 25166080 | tf_op jit(solution)/shard_map/while/body/eval_jaxpr/scatter-add | solution.py:32
  122.2 2.8 gather_fusion
  125.0 7.4 broadcast_multiply_fusion.5
  132.5 19.6 %scatter_fusion = f32[96,128,256]{2,1,0:T(8,128)} fusion(f32[96,128,256]{2,1,0:T(8,128)} %get-tuple-element.258, s32[64]{0:T(128)S(1)} %dynamic_slice.49, f32[64,128,256]{2,1,0:T(8,128)} %broadcast_multiply_fusion.5), kind=kCustom, calls=%fused_computation.2.clone.1 | custom fusion | flops 2097152 | bytes 25166080 | tf_op jit(solution)/shard_map/while/body/eval_jaxpr/scatter-add | solution.py:32
  153.4 2.8 gather_fusion
  156.3 7.4 broadcast_multiply_fusion.5
  163.7 19.6 %scatter_fusion = f32[96,128,256]{2,1,0:T(8,128)} fusion(f32[96,128,256]{2,1,0:T(8,128)} %get-tuple-element.258, s32[64]{0:T(128)S(1)} %dynamic_slice.49, f32[64,128,256]{2,1,0:T(8,128)} %broadcast_multiply_fusion.5), kind=kCustom, calls=%fused_computation.2.clone.1 | custom fusion | flops 2097152 | bytes 25166080 | tf_op jit(solution)/shard_map/while/body/eval_jaxpr/scatter-add | solution.py:32
  183.3 8.1 %convert_element_type.55 = bf16[96,128,256]{2,1,0:T(8,128)(2,1)} convert(f32[96,128,256]{2,1,0:T(8,128)} %get-tuple-element.87) | non-fusion elementwise | flops 3145728 | bytes 18874368 | tf_op jit(solution)/shard_map/convert_element_type | solution.py:70
  192.1 143.2 %reduce-scatter.3.cloned.1.call-done = bf16[384,256]{1,0:T(8,128)(2,1)} async-done(((bf16[12288,256]{1,0:T(8,128)(2,1)}), bf16[384,256]{1,0:T(8,128)(2,1)}) %reduce-scatter.3.cloned.1.call-update) | async-done | bytes 196624 | tf_op jit(solution)/shard_map/reduce_scatter | solution.py:69
  335.3 2.0 multiply_convert_fusion
  338.3 8.7 %copy.11 = bf16[1,1,192,128,128]{3,4,2,1,0:T(8,128)(2,1)} copy(bf16[1,1,192,128,128]{4,3,2,1,0:T(8,128)(2,1)} %bitcast.24) | data formatting | bytes 12582912 | tf_op args[5]
  348.1 58.3 %all-gather.5.cloned.1.call-done = bf16[12288,256]{1,0:T(8,128)(2,1)} async-done(((bf16[384,256]{1,0:T(8,128)(2,1)}), bf16[12288,256]{1,0:T(8,128)(2,1)}) %all-gather.5.cloned.1.call-update) | async-done | bytes 6291472 | tf_op jit(solution)/shard_map/all_gather | solution.py:88
  406.8 80.9 %while.21 = (s32[]{:T(128)}, f32[24,128,256]{2,1,0:T(8,128)S(1)}, s32[3]{0:T(128)S(1)}, s32[192]{0:T(256)S(1)}, bf16[192,128,128]{1,2,0:T(8,128)(2,1)}, /*index=...) while((s32[]{:T(128)}, f32[24,128,256]{2,1,0:T(8,128)S(1)}, ...), condition=%wide.region_6.7_spmd, body=%wide.region_4.6_spmd.sunk | while | flops 543163776 | bytes 48241472 | solution.py:36
  408.2 5.6 gather_fusion.1
  413.8 7.4 broadcast_multiply_fusion.6
  421.3 12.5 %scatter_fusion.1 = f32[24,128,256]{2,1,0:T(8,128)S(1)} fusion(f32[24,128,256]{2,1,0:T(8,128)S(1)} %get-tuple-element.294, s32[64]{0:T(128)S(1)} %dynamic_slice.53, f32[64,128,256]{2,1,0:T(8,128)} %broadcast_multiply_fusion.6), kind=kCustom, calls=%fused_computation.3.clone.1 | custom fusion | flops 2097152 | bytes 25166080 | tf_op jit(solution)/shard_map/while/body/eval_jaxpr/scatter-add | solution.py:32
  435.1 5.6 gather_fusion.1
  440.8 7.4 broadcast_multiply_fusion.6
  448.3 12.5 %scatter_fusion.1 = f32[24,128,256]{2,1,0:T(8,128)S(1)} fusion(f32[24,128,256]{2,1,0:T(8,128)S(1)} %get-tuple-element.294, s32[64]{0:T(128)S(1)} %dynamic_slice.53, f32[64,128,256]{2,1,0:T(8,128)} %broadcast_multiply_fusion.6), kind=kCustom, calls=%fused_computation.3.clone.1 | custom fusion | flops 2097152 | bytes 25166080 | tf_op jit(solution)/shard_map/while/body/eval_jaxpr/scatter-add | solution.py:32
  462.1 5.6 gather_fusion.1
  467.8 7.4 broadcast_multiply_fusion.6
  475.3 12.5 %scatter_fusion.1 = f32[24,128,256]{2,1,0:T(8,128)S(1)} fusion(f32[24,128,256]{2,1,0:T(8,128)S(1)} %get-tuple-element.294, s32[64]{0:T(128)S(1)} %dynamic_slice.53, f32[64,128,256]{2,1,0:T(8,128)} %broadcast_multiply_fusion.6), kind=kCustom, calls=%fused_computation.3.clone.1 | custom fusion | flops 2097152 | bytes 25166080 | tf_op jit(solution)/shard_map/while/body/eval_jaxpr/scatter-add | solution.py:32
  489.2 173.0 %all-reduce.2.cloned.1.call-done = f32[256,256]{1,0:T(8,128)} async-done(((f32[256,256]{1,0:T(8,128)}), f32[256,256]{1,0:T(8,128)}) %all-reduce.2.cloned.1.call-update) | async-done | bytes 262160 | tf_op jit(solution)/shard_map/psum | solution.py:83
  662.3 1.7 broadcast_multiply_fusion.2
  663.9 91.3 %reduce-scatter.5.cloned.1.call-done = bf16[384,256]{1,0:T(8,128)(2,1)} async-done(((bf16[3072,256]{1,0:T(8,128)(2,1)}), bf16[384,256]{1,0:T(8,128)(2,1)}) %reduce-scatter.5.cloned.1.call-update) | async-done | bytes 196624 | tf_op jit(solution)/shard_map/reduce_scatter | solution.py:99
  755.2 1.8 fusion.20
  (70 shorter events, 12.1 us)
Async XLA Ops:
  7.2 328.1 %copy-start = (bf16[256,256]{1,0:T(8,128)(2,1)S(1)}, bf16[256,256]{1,0:T(8,128)(2,1)}, u32[]{:S(2)}) copy-start(bf16[256,256]{1,0:T(8,128)(2,1)} %param.13) | copy-start | bytes 393220
  7.2 76.2 %all-gather.3.cloned.1.call-start = ((), (), s32[]{:S(2)}) async-start(), calls=%async_computation.2 | async-start | bytes 1769472 | tf_op jit(solution)/shard_map/all_gather | solution.py:58
  8.5 0.5 copy-start.5
  10.8 324.5 %reduce-scatter.3.cloned.1.call-start = ((), (), s32[]{:S(2)}) async-start(), calls=%async_computation.3 | async-start | bytes 6488064 | tf_op jit(solution)/shard_map/reduce_scatter | solution.py:69
  83.4 6.1 copy-start.2
  191.4 0.7 copy-start.8
  191.5 143.8 %copy-start.9 = (bf16[384,256]{1,0:T(8,128)(2,1)S(1)}, bf16[384,256]{1,0:T(8,128)(2,1)}, u32[]{:S(2)}) copy-start(bf16[384,256]{1,0:T(8,128)(2,1)} %param.14) | copy-start | bytes 589828
  191.5 215.0 %all-gather.5.cloned.1.call-start = ((), (), s32[]{:S(2)}) async-start(), calls=%async_computation.4 | async-start | bytes 6488064 | tf_op jit(solution)/shard_map/all_gather | solution.py:88
  338.2 8.8 %copy-start.4 = (bf16[384,256]{1,0:T(8,128)(2,1)S(1)}, bf16[384,256]{1,0:T(8,128)(2,1)}, u32[]{:S(2)}) copy-start(bf16[384,256]{1,0:T(8,128)(2,1)} %reduce-scatter.3.cloned.1.call-done) | copy-start | bytes 589828
  338.3 324.0 %all-reduce.2.cloned.1.call-start = ((), (), s32[]{:S(2)}) async-start(), calls=%async_computation.6 | async-start | bytes 524288 | tf_op jit(solution)/shard_map/psum | solution.py:83
  348.1 407.1 %reduce-scatter.5.cloned.1.call-start = ((), (), s32[]{:S(2)}) async-start(), calls=%async_computation.5 | async-start | bytes 1769472 | tf_op jit(solution)/shard_map/reduce_scatter | solution.py:99
  487.8 267.5 %copy-start.3 = (bf16[384,256]{1,0:T(8,128)(2,1)S(1)}, bf16[384,256]{1,0:T(8,128)(2,1)}, u32[]{:S(2)}) copy-start(bf16[384,256]{1,0:T(8,128)(2,1)} %param.12) | copy-start | bytes 589828
  487.8 267.5 %copy-start.6 = (f32[384]{0:T(512)S(1)}, f32[384]{0:T(512)}, u32[]{:S(2)}) copy-start(f32[384]{0:T(512)} %copy-done.5) | copy-start | bytes 4612
  487.8 267.5 %copy-start.7 = (f32[384]{0:T(512)S(1)}, f32[384]{0:T(512)}, u32[]{:S(2)}) copy-start(f32[384]{0:T(512)} %get-tuple-element.135) | copy-start | bytes 4612
  487.8 269.3 %copy-start.1 = (bf16[256,256]{1,0:T(8,128)(2,1)S(1)}, bf16[256,256]{1,0:T(8,128)(2,1)}, u32[]{:S(2)}) copy-start(bf16[256,256]{1,0:T(8,128)(2,1)} %param.13) | copy-start | bytes 393220
Sparse Core Ops, SparseCore 0:
  11.2 72.1 all-gather.2
  191.6 143.6 reduce-scatter.2
  338.4 68.0 all-gather.4
  412.4 249.8 all-reduce.1
  666.2 89.0 reduce-scatter.4
where the time goes:
time: 765 us; the launch traced here: 764 us
  waiting for transfers between devices  537 us (70%)
  other arithmetic  113 us (15%)
  matrix products  48.2 us (6%)
  local copies, waits for them, and re-layouts  46.6 us (6%)
  between operations  14.5 us (2%)
    psum x1, waiting for transfers between devices, per_device(): lax.psum(local_weight, ('row', 'col')) / math.sqrt(total_nodes)  173 us
    reduce_scatter x1, waiting for transfers between devices, per_device(): lax.psum_scatter(forward_terms.astype(jnp.bfloat16), 'col', scatter_dimen...  143 us
    scatter-add x6, other arithmetic, advance(): jax.ops.segment_sum(products, targets, num_segments=out_count)  96.4 us
    reduce_scatter x1, waiting for transfers between devices, per_device(): lax.psum_scatter(backward_terms.astype(jnp.bfloat16), 'row', scatter_dime...  91.3 us
    all_gather x1, waiting for transfers between devices, per_device(): source_block = lax.all_gather(scaled, 'row', axis=0, tiled=True)  71.1 us
    all_gather x1, waiting for transfers between devices, per_device(): upstream_block = lax.all_gather(upstream, 'col', axis=0, tiled=True)  58.3 us
    gather x6, local copies, waits for them, and re-layouts, advance(): picked = jnp.take(lookup, chosen, axis=0)  25.2 us
    dot_general x3, matrix products, advance(): jnp.einsum('tij,tif->tjf', block_tiles, picked, preferred_element_type=jn...  22.2 us
  transfers between devices with their start and end apart: 5, of which 5 were waited for; matrix products, arithmetic and copies ran while one was open for 12% of the time, Pallas kernels for 0%

commit v1 on v0

v1 whole, which is shorter than its diff:
```python
import functools
import math

import jax
import jax.numpy as jnp
from jax import lax
from jax.experimental import pallas as pl
from jax.experimental.pallas import tpu as pltpu
from jax.sharding import PartitionSpec as P

decay_rate = 0.01
f32 = jnp.float32
bf16 = jnp.bfloat16

chunks = ((0, 1, 2),)
unroll = 16
padded = 256

x_bit, z_bit, y_bit = 1, 3, 1


def exchange(value, axis, mask):
    size = lax.axis_size(axis)
    return lax.ppermute(value, axis, [(i, i ^ mask) for i in range(size)])


def group_kernel(table, tiles, source, *rest, group, flipped, carried):
    previous = rest[0] if carried else None
    out = rest[-1]

    def clear(i, _):
        if carried:
            out[i] = previous[i].astype(out.dtype)
        else:
            out[i] = jnp.zeros(out.shape[1:], out.dtype)
        return 0

    lax.fori_loop(0, out.shape[0], clear, 0)
    slots = tiles.shape[0]
    start = table[slots + group]
    stop = table[slots + group + 1]
    dims = (((0,), (0,)), ((), ())) if flipped else (((1,), (0,)), ((), ()))

    def advance(number, total):
        for step in range(unroll):
            index = start + number * unroll + step
            real = index < stop
            entry = table[jnp.minimum(index, stop - 1)]
            slot = entry & 255
            place = (entry >> 8) & 255
            origin = (entry >> 16) & 255
            fresh = jnp.logical_and(real, (entry >> 24) == 1)
            product = lax.dot_general(
                tiles[slot], source[origin], dims, preferred_element_type=f32
            )
            product = product * real.astype(f32)
            if carried:
                total = jnp.where(fresh, previous[place], total) + product
            else:
                total = total * (1.0 - fresh.astype(f32)) + product
            out[place] = total.astype(out.dtype)
        return total

    steps = (stop - start + unroll - 1) // unroll
    lax.fori_loop(0, steps, advance, jnp.zeros(out.shape[1:], f32))


def group_products(table, tiles, source, count, group, flipped, previous=None, dtype=bf16):
    slots, edge, _ = tiles.shape
    width = source.shape[2]
    operands = (table, tiles, source) + (() if previous is None else (previous,))
    whole = pl.BlockSpec(memory_space=pltpu.VMEM)
    return pl.pallas_call(
        functools.partial(
            group_kernel, group=group, flipped=flipped, carried=previous is not None
        ),
        out_shape=jax.ShapeDtypeStruct((count, edge, width), dtype),
        in_specs=[pl.BlockSpec(memory_space=pltpu.SMEM)] + [whole] * (len(operands) - 1),
        out_specs=whole,
        compiler_params=pltpu.CompilerParams(vmem_limit_bytes=40 << 20),
        cost_estimate=pl.CostEstimate(
            flops=2 * count * edge * edge * width,
            bytes_accessed=count * edge * width * 2,
            transcendentals=0,
        ),
        name=("backward" if flipped else "forward") + str(group),
    )(*operands)


def slot_table(key, place, origin, groups):
    slots = key.shape[0]
    number = jnp.arange(slots, dtype=jnp.int32)
    earlier = number[None, :] < number[:, None]
    same = key[None, :] == key[:, None]
    ahead = jnp.logical_or(key[None, :] < key[:, None], jnp.logical_and(same, earlier))
    rank = jnp.sum(ahead.astype(jnp.int32), axis=1)
    repeats = jnp.sum(jnp.logical_and(same, earlier).astype(jnp.int32), axis=1)
    fresh = (repeats == 0).astype(jnp.int32)
    packed = number | (place << 8) | (origin << 16) | (fresh << 24)
    hit = rank[None, :] == number[:, None]
    ordered = jnp.sum(jnp.where(hit, packed[None, :], 0), axis=1)
    limits = jnp.arange(padded - slots, dtype=jnp.int32) * 128
    bounds = jnp.sum((key[None, :] < limits[:, None]).astype(jnp.int32), axis=1)
    live = jnp.sum((key < groups * 128).astype(jnp.int32))
    return jnp.concatenate([ordered, jnp.minimum(bounds, live)])


def slot_tables(coords, live_count, own_col, own_row, per_owner):
    tile_row = coords[:, 0]
    tile_col = coords[:, 1]
    alive = jnp.arange(coords.shape[0], dtype=jnp.int32) < live_count
    apart = (tile_row // per_owner) ^ own_col
    part = tile_row % per_owner
    core = apart & 1
    x = (apart >> x_bit) & 3
    z = (apart >> z_bit) & 3
    low = jnp.where(x == 0, 8, jnp.where(x == 1, 0, jnp.where(x == 2, 2, 10)))
    high = jnp.where(x == 0, 12, jnp.where(x == 1, 14, jnp.where(x == 2, 4, 6)))
    block = jnp.where(z < 2, low, high) + (z & 1)
    later = block // 8
    chunk = jnp.zeros_like(part)
    inner = jnp.zeros_like(part)
    breadth = jnp.zeros_like(part)
    for k, members in enumerate(chunks):
        for i, member in enumerate(members):
            chunk = jnp.where(part == member, k, chunk)
            inner = jnp.where(part == member, i, inner)
            breadth = jnp.where(part == member, len(members), breadth)
    row_apart = (tile_col // per_owner) ^ own_row
    source_place = ((row_apart & 1) * 4 + (row_apart >> y_bit)) * per_owner + tile_col % per_owner
    forward_place = (block & 7) * breadth + inner
    forward_key = (chunk * 4 + later * 2 + 1 - core) * 128 + forward_place
    backward_origin = (core * 16 + x * 4 + z) * breadth + inner
    backward_key = chunk * 128 + source_place
    dead = 1 << 20

    def table(key, place, origin, groups):
        return slot_table(
            jnp.where(alive, key, dead),
            jnp.where(alive, place, 0),
            jnp.where(alive, origin, 0),
            groups,
        )

    forward = table(forward_key, forward_place, source_place, 4 * len(chunks))
    backward = table(backward_key, source_place, backward_origin, len(chunks))
    return forward, backward


def ring_gather(block, axis, bit):
    near, far = 1 << bit, 3 << bit
    half = block.shape[0] // 2
    first = exchange(block, axis, near)
    third = exchange(block, axis, far)
    second_low = exchange(first[:half], axis, far)
    second_high = exchange(third[half:], axis, near)
    return [block, first, second_low, second_high, third]


def wide(value):
    return value.astype(f32)


def reduce_row(terms):
    near, far = 1 << y_bit, 3 << y_bit
    low, high = terms[0], terms[1]
    low_in = exchange(low[1:3], "row", near)
    high_in = exchange(high[2:4], "row", far)
    low_next = exchange((wide(low[3]) + wide(low_in[1])).astype(bf16), "row", far)
    high_next = exchange((wide(high[1]) + wide(high_in[0])).astype(bf16), "row", near)
    leaving = (wide(high[0]) + wide(high_in[1]) + wide(high_next)).astype(bf16)
    arrived = exchange(leaving, "row", 1)
    return wide(low[0]) + wide(low_in[0]) + wide(low_next) + wide(arrived)


def reduce_weight(term, own_col):
    rows = term.shape[0]
    half, eighth = rows // 2, rows // 8
    core = own_col & 1
    x = (own_col >> x_bit) & 3
    mine = lax.dynamic_slice_in_dim(term, core * half, half, 0)
    other = lax.dynamic_slice_in_dim(term, (1 - core) * half, half, 0)
    mine = mine + exchange(other, "col", 1)
    share = lax.dynamic_slice_in_dim(mine, x * eighth, eighth, 0)
    for distance in (1, 2, 3):
        piece = lax.dynamic_slice_in_dim(mine, (x ^ distance) * eighth, eighth, 0)
        share = share + exchange(piece, "col", distance << x_bit)
    for axis, mask in (("col", 1 << z_bit), ("col", 2 << z_bit), ("row", 1 << y_bit), ("row", 3 << y_bit), ("row", 1)):
        share = share + exchange(share, axis, mask)
    total = jnp.zeros((half, term.shape[1]), f32)
    total = lax.dynamic_update_slice_in_dim(total, share, x * eighth, 0)
    for distance in (1, 2, 3):
        piece = exchange(share, "col", distance << x_bit)
        total = lax.dynamic_update_slice_in_dim(total, piece, (x ^ distance) * eighth, 0)
    other = exchange(total, "col", 1)
    lower = jnp.where(core == 0, total, other)
    upper = jnp.where(core == 0, other, total)
    return jnp.concatenate([lower, upper], axis=0)


def per_device(
    embedding, weight, grad_out, in_degree, out_degree, tile_edges, tile_coords, tile_count
):
    tiles = tile_edges[0, 0]
    n_row = lax.axis_size("row")
    n_col = lax.axis_size("col")
    own_row = lax.axis_index("row").astype(jnp.int32)
    own_col = lax.axis_index("col").astype(jnp.int32)
    own_rows, width = embedding.shape
    edge = tiles.shape[1]
    per_owner = own_rows // edge
    total_nodes = own_rows * n_row * n_col
    forward_table, backward_table = slot_tables(
        tile_coords[0, 0], tile_count[0, 0], own_col, own_row, per_owner
    )

    scale_out = lax.rsqrt(out_degree.astype(f32))
    scale_in = lax.rsqrt(in_degree.astype(f32))
    scaled = (scale_out[:, None] * wide(embedding)).astype(bf16)
    gathered = ring_gather(scaled, "row", y_bit)
    gathered += ring_gather(exchange(scaled, "row", 1), "row", y_bit)
    source = jnp.concatenate(gathered, axis=0).reshape(n_row * per_owner, edge, width)

    near, far = 1 << x_bit, 3 << x_bit
    upstream_parts = []
    hidden_parts = []
    local_weight = jnp.zeros((width, width), f32)
    for k, members in enumerate(chunks):
        count = 8 * len(members)
        rows = len(members) * edge

        def products(group):
            return group_products(forward_table, tiles, source, count, 4 * k + group, False)

        def blocks(value):
            return value.reshape(8, rows, width)

        leaving = products(0)
        early_in = blocks(exchange(leaving, "col", 1))
        early = blocks(products(1))
        leaving = products(2)
        late_in = blocks(exchange(leaving, "col", 1))
        late = blocks(products(3))

        def first_sum(low, high):
            return (wide(early[low:high]) + wide(early_in[low:high])).astype(bf16)

        def late_sum(low, high):
            return wide(late[low:high]) + wide(late_in[low:high])

        low_in = exchange(first_sum(0, 4), "col", near)
        high_in = exchange(first_sum(4, 8), "col", far)
        low_next = exchange((late_sum(2, 4) + wide(low_in[2:4])).astype(bf16), "col", far)
        high_next = exchange((late_sum(6, 8) + wide(high_in[0:2])).astype(bf16), "col", near)
        low = late_sum(0, 2) + wide(low_in[0:2]) + wide(low_next)
        high = late_sum(4, 6) + wide(high_in[2:4]) + wide(high_next)
        summed = low[0]
        for distance, leaving in ((1, low[1]), (2, high[0]), (3, high[1])):
            summed = summed + wide(
                exchange(leaving.astype(bf16), "col", distance << z_bit)
            )

        def own(value):
            return jnp.concatenate([value[m * edge : (m + 1) * edge] for m in members], axis=0)

        chunk_scale = own(scale_in)
        aggregate = (chunk_scale[:, None] * summed).astype(bf16)
        preact = jnp.dot(aggregate, weight, preferred_element_type=f32)
        gates = jax.nn.sigmoid(preact)
        hidden_parts.append((preact * gates).astype(bf16))
        delta = (wide(own(grad_out)) * gates * (1.0 + preact * (1.0 - gates))).astype(bf16)
        local_weight = local_weight + lax.dot_general(
            aggregate, delta, (((0,), (0,)), ((), ())), preferred_element_type=f32
        )
        projected = lax.dot_general(
            delta, weight, (((1,), (1,)), ((), ())), preferred_element_type=f32
        )
        upstream = (chunk_scale[:, None] * projected).astype(bf16)
        stack = [upstream] + [
            exchange(upstream, "col", distance << z_bit) for distance in (1, 2, 3)
        ]
        upstream_parts.append(jnp.concatenate(stack, axis=0))

    hidden = jnp.concatenate(hidden_parts, axis=0)
    grad_weight = reduce_weight(local_weight, own_col) / math.sqrt(total_nodes)

    terms = None
    for k, members in enumerate(chunks):
        pieces = ring_gather(upstream_parts[k], "col", x_bit)
        pieces += [exchange(piece, "col", 1) for piece in pieces]
        block = jnp.concatenate(pieces, axis=0).reshape(n_col * len(members), edge, width)
        last = k == len(chunks) - 1
        terms = group_products(
            backward_table,
            tiles,
            block,
            n_row * per_owner,
            k,
            True,
            terms,
            bf16 if last else f32,
        )
    source_total = reduce_row(terms.reshape(2, 4, own_rows, width))
    decay = decay_rate * jnp.sqrt(out_degree.astype(f32))
    grad_embedding = scale_out[:, None] * source_total + decay[:, None] * wide(embedding)
    return (hidden, grad_embedding, grad_weight)


def solution(mesh):
    in_specs = (
        P(("col", "row"), None),
        P(),
        P(("row", "col"), None),
        P(("row", "col")),
        P(("col", "row")),
        P("row", "col", None, None, None),
        P("row", "col", None, None),
        P("row", "col"),
    )
    out_specs = (P(("row", "col"), None), P(("col", "row"), None), P())
    return jax.shard_map(
        per_device, mesh=mesh, in_specs=in_specs, out_specs=out_specs, check_vma=False
    )
```

time: 765 us -> 213 us (0.28)
  waiting for transfers between devices: 537 us -> 89.7 us
  other arithmetic: 113 us -> 14.4 us
  starting transfers between devices: 0.2 us -> 69.4 us
  matrix products: 48.2 us -> 2.22 us
  local copies, waits for them, and re-layouts: 46.6 us -> 16 us
  Pallas kernels: 0 us -> 15 us
  between operations: 14.5 us -> 1.83 us
    reduce_scatter x2 -> x0, waiting for transfers between devices: 234 us -> none  [the longest x1 143 us: per_device(): lax.psum_scatter(forward_terms.astype(jnp.bfloat16), 'col', scatter_dimen...]
    psum x1 -> x0, waiting for transfers between devices: 173 us -> none  [per_device(): lax.psum(local_weight, ('row', 'col')) / math.sqrt(total_nodes)]
    all_gather x2 -> x0, waiting for transfers between devices: 129 us -> none  [the longest x1 71.1 us: per_device(): source_block = lax.all_gather(scaled, 'row', axis=0, tiled=True)]
    scatter-add x6 -> x0, other arithmetic: 96.4 us -> none  [advance(): jax.ops.segment_sum(products, targets, num_segments=out_count)]
    ppermute x0 -> x48, waiting for transfers between devices: none -> 89.7 us  [exchange(): return lax.ppermute(value, axis, [(i, i ^ mask) for i in range(size)])]
    ppermute x0 -> x48, starting transfers between devices: none -> 69.4 us  [exchange(): return lax.ppermute(value, axis, [(i, i ^ mask) for i in range(size)])]
    dot_general x9 -> x3, matrix products: 48.2 us -> 2.22 us  [the longest x1 1.03 us: per_device(): preact = jnp.dot(aggregate, weight, preferred_element_type=f32)]
    gather x6 -> x0, local copies, waits for them, and re-layouts: 25.2 us -> none  [advance(): picked = jnp.take(lookup, chosen, axis=0)]
  transfers between devices with their start and end apart: 5 -> 48, of which waited for: 5 -> 22; matrix products, arithmetic and copies ran while one was open for 12% -> 11% of each run, Pallas kernels for 0% -> 6%
where the time goes in v1:
time: 213 us; the launch traced here: 209 us
  waiting for transfers between devices  89.7 us (42%)
  starting transfers between devices  69.4 us (33%)
  local copies, waits for them, and re-layouts  16 us (8%)
  Pallas kernels  15 us (7%)
  other arithmetic  14.4 us (7%)
  matrix products  2.22 us (1%)
    ppermute x48, waiting for transfers between devices, exchange(): return lax.ppermute(value, axis, [(i, i ^ mask) for i in range(size)])  89.7 us
    ppermute x48, starting transfers between devices, exchange(): return lax.ppermute(value, axis, [(i, i ^ mask) for i in range(size)])  69.4 us
    pallas_call x5, Pallas kernels, group_products(): pl.pallas_call(functools.partial(group_kernel, group=group, flipped=flipp...  15 us
    unnamed x39, local copies, waits for them, and re-layouts  14.7 us
  transfers between devices with their start and end apart: 48, of which 22 were waited for; matrix products, arithmetic and copies ran while one was open for 11% of the time, Pallas kernels for 6%

profile of v1, /device:TPU:2, one launch (start us, length us, event | category | flops | bytes accessed | tf_op | source)
XLA Modules:
  0.0 208.6 jit_solution(5141389921489641039)
XLA Ops:
  4.1 2.2 %collective-permute-start.2 = (bf16[384,256]{1,0:T(8,128)(2,1)S(1)}, bf16[384,256]{1,0:T(8,128)(2,1)S(1)}, u32[]{:S(2)}, u32[]{:S(2)}) collective-permute-start(bf16[384,256]{1,0:T(8,128)(2,1)S(1)} %get-tuple-element.21), channel_id=1, source_target_pairs={{0,192},{32,224},{64,128},{96,160},{128,64},{160,96},{192,0},{224,... | collective-permute-start | bytes 589832 | tf_op jit(solution)/shard_map/ppermute | solution.py:24
  6.3 7.2 %collective-permute-start.4 = (bf16[384,256]{1,0:T(8,128)(2,1)S(1)}, bf16[384,256]{1,0:T(8,128)(2,1)S(1)}, u32[]{:S(2)}, u32[]{:S(2)}) collective-permute-start(bf16[384,256]{1,0:T(8,128)(2,1)S(1)} %get-tuple-element.21), channel_id=1, source_target_pairs={{0,32},{32,0},{64,96},{96,64},{128,160},{160,128},{192,224},{224,1... | collective-permute-start | bytes 589832 | tf_op jit(solution)/shard_map/ppermute | solution.py:24
  21.8 2.2 %collective-permute-start.7 = (bf16[384,256]{1,0:T(8,128)(2,1)S(1)}, bf16[384,256]{1,0:T(8,128)(2,1)S(1)}, u32[]{:S(2)}, u32[]{:S(2)}) collective-permute-start(bf16[384,256]{1,0:T(8,128)(2,1)S(1)} %collective-permute-done.4), channel_id=1, source_target_pairs={{0,192},{32,224},{64,128},{96,160},{128,64},{160,96},{192,0},{224,... | collective-permute-start | bytes 589832 | tf_op jit(solution)/shard_map/ppermute | solution.py:24
  27.4 2.3 %collective-permute-start.6 = (bf16[192,256]{1,0:T(8,128)(2,1)S(1)}, bf16[192,256]{1,0:T(8,128)(2,1)S(1)}, u32[]{:S(2)}, u32[]{:S(2)}) collective-permute-start(bf16[192,256]{1,0:T(8,128)(2,1)S(1)} %slice.201), channel_id=1, source_target_pairs={{0,192},{32,224},{64,128},{96,160},{128,64},{160,96},{192,0},{224,... | collective-permute-start | bytes 294920 | tf_op jit(solution)/shard_map/ppermute | solution.py:24
  29.9 3.4 %collective-permute-done.6 = bf16[192,256]{1,0:T(8,128)(2,1)S(1)} collective-permute-done((bf16[192,256]{1,0:T(8,128)(2,1)S(1)}, bf16[192,256]{1,0:T(8,128)(2,1)S(1)}, u32[]{:S(2)}, u32[]{:S(2)}) %collective-permute-start.6) | collective-permute-done | bytes 98336 | tf_op jit(solution)/shard_map/ppermute | solution.py:24
  34.5 2.8 %copy-done.1 = bf16[1,1,192,128,128]{4,3,2,1,0:T(8,128)(2,1)S(1)} copy-done((bf16[1,1,192,128,128]{4,3,2,1,0:T(8,128)(2,1)S(1)}, bf16[1,1,192,128,128]{4,3,2,1,0:T(8,128)(2,1)}, u32[]{:S(2)}) %copy-start.1) | copy-done | bytes 6291480
  39.4 2.5 %forward2.1 = bf16[24,128,256]{2,1,0:T(8,128)(2,1)S(1)} custom-call(s32[256]{0:T(256)S(1)} %pad_add_fusion.table, bf16[192,128,128]{2,1,0:T(8,128)(2,1)S(1)} %bitcast.99, bf16[24,128,256]{2,1,0:T(8,128)(2,1)S(1)} %bitcast.106), custom_call_target="tpu_custom_call" | custom-call | flops 201326592 | bytes 1572864 | tf_op jit(solution)/shard_map/forward2/pallas_call | solution.py:73
  44.6 3.3 %collective-permute-start.11 = (bf16[4,384,256]{2,1,0:T(8,128)(2,1)S(1)}, bf16[4,384,256]{2,1,0:T(8,128)(2,1)}, u32[]{:S(2)}, u32[]{:S(2)}) collective-permute-start(bf16[4,384,256]{2,1,0:T(8,128)(2,1)S(1)} %bitcast.114), channel_id=1, source_target_pairs={{0,2},{1,3},{2,0},{3,1},{4,6},{5,7},{6,4},{7,5},{8,10},{9,11},{10,... | collective-permute-start | bytes 2359304 | tf_op jit(solution)/shard_map/ppermute | solution.py:24
  50.4 14.1 %collective-permute-done.14 = bf16[4,384,256]{2,1,0:T(8,128)(2,1)S(1)} collective-permute-done((bf16[4,384,256]{2,1,0:T(8,128)(2,1)S(1)}, bf16[4,384,256]{2,1,0:T(8,128)(2,1)S(1)}, u32[]{:S(2)}, u32[]{:S(2)}) %collective-permute-start.14) | collective-permute-done | bytes 786464 | tf_op jit(solution)/shard_map/ppermute | solution.py:24
  67.8 2.6 %collective-permute-start.12 = (bf16[2,384,256]{2,1,0:T(8,128)(2,1)S(1)}, bf16[2,384,256]{2,1,0:T(8,128)(2,1)S(1)}, u32[]{:S(2)}, u32[]{:S(2)}) collective-permute-start(bf16[2,384,256]{2,1,0:T(8,128)(2,1)S(1)} %fusion.4), channel_id=1, source_target_pairs={{0,6},{1,7},{2,4},{3,5},{4,2},{5,3},{6,0},{7,1},{8,14},{9,15},{10,... | collective-permute-start | bytes 1179656 | tf_op jit(solution)/shard_map/ppermute | solution.py:24
  70.4 6.2 %collective-permute-done.15 = bf16[2,384,256]{2,1,0:T(8,128)(2,1)} collective-permute-done((bf16[2,384,256]{2,1,0:T(8,128)(2,1)}, bf16[2,384,256]{2,1,0:T(8,128)(2,1)}, u32[]{:S(2)}, u32[]{:S(2)}) %collective-permute-start.15) | collective-permute-done | bytes 393248 | tf_op jit(solution)/shard_map/ppermute | solution.py:24
  82.7 9.7 %collective-permute-done.16 = bf16[384,256]{1,0:T(8,128)(2,1)S(1)} collective-permute-done((bf16[384,256]{1,0:T(8,128)(2,1)S(1)}, bf16[384,256]{1,0:T(8,128)(2,1)S(1)}, u32[]{:S(2)}, u32[]{:S(2)}) %collective-permute-start.16) | collective-permute-done | bytes 196640 | tf_op jit(solution)/shard_map/ppermute | solution.py:24
  92.4 2.3 %collective-permute-done.13 = bf16[384,256]{1,0:T(8,128)(2,1)S(1)} collective-permute-done((bf16[384,256]{1,0:T(8,128)(2,1)S(1)}, bf16[384,256]{1,0:T(8,128)(2,1)S(1)}, u32[]{:S(2)}, u32[]{:S(2)}) %collective-permute-start.13) | collective-permute-done | bytes 196640 | tf_op jit(solution)/shard_map/ppermute | solution.py:24
  98.2 2.5 %collective-permute-start.37 = (f32[32,256]{1,0:T(8,128)S(1)}, f32[32,256]{1,0:T(8,128)S(1)}, u32[]{:S(2)}, u32[]{:S(2)}) collective-permute-start(f32[32,256]{1,0:T(8,128)S(1)} %get-tuple-element.47), channel_id=1, source_target_pairs={{0,4},{1,5},{2,6},{3,7},{4,0},{5,1},{6,2},{7,3},{8,12},{9,13},{10,... | collective-permute-start | bytes 98312 | tf_op jit(solution)/shard_map/ppermute | solution.py:24
  107.7 4.4 %collective-permute-done.18 = bf16[384,256]{1,0:T(8,128)(2,1)S(1)} collective-permute-done((bf16[384,256]{1,0:T(8,128)(2,1)S(1)}, bf16[384,256]{1,0:T(8,128)(2,1)S(1)}, u32[]{:S(2)}, u32[]{:S(2)}) %collective-permute-start.18) | collective-permute-done | bytes 196640 | tf_op jit(solution)/shard_map/ppermute | solution.py:24
  112.1 9.1 %collective-permute-done.19 = bf16[384,256]{1,0:T(8,128)(2,1)S(1)} collective-permute-done((bf16[384,256]{1,0:T(8,128)(2,1)S(1)}, bf16[384,256]{1,0:T(8,128)(2,1)S(1)}, u32[]{:S(2)}, u32[]{:S(2)}) %collective-permute-start.19) | collective-permute-done | bytes 196640 | tf_op jit(solution)/shard_map/ppermute | solution.py:24
  121.3 2.3 %collective-permute-start.21 = (bf16[1536,256]{1,0:T(8,128)(2,1)S(1)}, bf16[1536,256]{1,0:T(8,128)(2,1)S(1)}, u32[]{:S(2)}, u32[]{:S(2)}) collective-permute-start(bf16[1536,256]{1,0:T(8,128)(2,1)S(1)} %pad_maximum_fusion), channel_id=1, source_target_pairs={{0,2},{1,3},{2,0},{3,1},{4,6},{5,7},{6,4},{7,5},{8,10},{9,11},{10,... | collective-permute-start | bytes 2359304 | tf_op jit(solution)/shard_map/ppermute | solution.py:24
  124.2 2.3 %collective-permute-start.23 = (bf16[1536,256]{1,0:T(8,128)(2,1)S(1)}, bf16[1536,256]{1,0:T(8,128)(2,1)S(1)}, u32[]{:S(2)}, u32[]{:S(2)}) collective-permute-start(bf16[1536,256]{1,0:T(8,128)(2,1)S(1)} %pad_maximum_fusion), channel_id=1, source_target_pairs={{0,6},{1,7},{2,4},{3,5},{4,2},{5,3},{6,0},{7,1},{8,14},{9,15},{10,... | collective-permute-start | bytes 2359304 | tf_op jit(solution)/shard_map/ppermute | solution.py:24
  126.6 3.4 %collective-permute-start.40 = (f32[32,256]{1,0:T(8,128)S(1)}, f32[32,256]{1,0:T(8,128)S(1)}, u32[]{:S(2)}, u32[]{:S(2)}) collective-permute-start(f32[32,256]{1,0:T(8,128)S(1)} %add.367), channel_id=1, source_target_pairs={{0,16},{1,17},{2,18},{3,19},{4,20},{5,21},{6,22},{7,23},{8,24},{9,... | collective-permute-start | bytes 98312 | tf_op jit(solution)/shard_map/ppermute | solution.py:24
  132.3 3.4 %collective-permute-done.41 = f32[32,256]{1,0:T(8,128)S(1)} collective-permute-done((f32[32,256]{1,0:T(8,128)S(1)}, f32[32,256]{1,0:T(8,128)S(1)}, u32[]{:S(2)}, u32[]{:S(2)}) %collective-permute-start.41) | collective-permute-done | bytes 32800 | tf_op jit(solution)/shard_map/ppermute | solution.py:24
  137.2 3.7 %collective-permute-done.42 = f32[32,256]{1,0:T(8,128)S(1)} collective-permute-done((f32[32,256]{1,0:T(8,128)S(1)}, f32[32,256]{1,0:T(8,128)S(1)}, u32[]{:S(2)}, u32[]{:S(2)}) %collective-permute-start.42) | collective-permute-done | bytes 32800 | tf_op jit(solution)/shard_map/ppermute | solution.py:24
  140.9 5.5 %collective-permute-start.43 = (f32[32,256]{1,0:T(8,128)S(1)}, f32[32,256]{1,0:T(8,128)S(1)}, u32[]{:S(2)}, u32[]{:S(2)}) collective-permute-start(f32[32,256]{1,0:T(8,128)S(1)} %add.370), channel_id=1, source_target_pairs={{0,32},{32,0},{64,96},{96,64},{128,160},{160,128},{192,224},{224,1... | collective-permute-start | bytes 98312 | tf_op jit(solution)/shard_map/ppermute | solution.py:24
  147.1 2.1 collective-permute-done.43
  152.1 2.3 %collective-permute-start.45 = (f32[32,256]{1,0:T(8,128)S(1)}, f32[32,256]{1,0:T(8,128)S(1)}, u32[]{:S(2)}, u32[]{:S(2)}) collective-permute-start(f32[32,256]{1,0:T(8,128)S(1)} %get-tuple-element.12), channel_id=1, source_target_pairs={{0,4},{1,5},{2,6},{3,7},{4,0},{5,1},{6,2},{7,3},{8,12},{9,13},{10,... | collective-permute-start | bytes 98312 | tf_op jit(solution)/shard_map/ppermute | solution.py:24
  155.8 2.2 %collective-permute-done.22 = bf16[768,256]{1,0:T(8,128)(2,1)S(1)} collective-permute-done((bf16[768,256]{1,0:T(8,128)(2,1)S(1)}, bf16[768,256]{1,0:T(8,128)(2,1)S(1)}, u32[]{:S(2)}, u32[]{:S(2)}) %collective-permute-start.22) | collective-permute-done | bytes 393248 | tf_op jit(solution)/shard_map/ppermute | solution.py:24
  158.7 3.6 %collective-permute-done.24 = bf16[768,256]{1,0:T(8,128)(2,1)S(1)} collective-permute-done((bf16[768,256]{1,0:T(8,128)(2,1)S(1)}, bf16[768,256]{1,0:T(8,128)(2,1)S(1)}, u32[]{:S(2)}, u32[]{:S(2)}) %collective-permute-start.24) | collective-permute-done | bytes 393248 | tf_op jit(solution)/shard_map/ppermute | solution.py:24
  169.8 2.8 %copy-done.2 = bf16[12288,256]{1,0:T(8,128)(2,1)S(1)} copy-done((bf16[12288,256]{1,0:T(8,128)(2,1)S(1)}, bf16[12288,256]{1,0:T(8,128)(2,1)}, u32[]{:S(2)}) %copy-start.2) | copy-done | bytes 6291480
  172.6 6.5 %backward0.1 = bf16[24,128,256]{2,1,0:T(8,128)(2,1)S(1)} custom-call(s32[256]{0:T(256)S(1)} %pad_add_fusion.1.table, bf16[192,128,128]{2,1,0:T(8,128)(2,1)S(1)} %bitcast.104, bf16[96,128,256]{2,1,0:T(8,128)(2,1)S(1)} %bitcast.109), custom_call_target="tpu_custom_call" | custom-call | flops 201326592 | bytes 1572864 | tf_op jit(solution)/shard_map/backward0/pallas_call | solution.py:73
  179.6 10.6 %collective-permute-done.32 = bf16[2,384,256]{2,1,0:T(8,128)(2,1)S(1)} collective-permute-done((bf16[2,384,256]{2,1,0:T(8,128)(2,1)S(1)}, bf16[2,384,256]{2,1,0:T(8,128)(2,1)S(1)}, u32[]{:S(2)}, u32[]{:S(2)}) %collective-permute-start.32) | collective-permute-done | bytes 393248 | tf_op jit(solution)/shard_map/ppermute | solution.py:24
  191.1 3.7 %collective-permute-start.31 = (bf16[384,256]{1,0:T(8,128)(2,1)S(1)}, bf16[384,256]{1,0:T(8,128)(2,1)S(1)}, u32[]{:S(2)}, u32[]{:S(2)}) collective-permute-start(bf16[384,256]{1,0:T(8,128)(2,1)S(1)} %fusion.16), channel_id=1, source_target_pairs={{0,192},{32,224},{64,128},{96,160},{128,64},{160,96},{192,0},{224,... | collective-permute-start | bytes 589832 | tf_op jit(solution)/shard_map/ppermute | solution.py:24
  196.2 5.4 %collective-permute-start.34 = (bf16[384,256]{1,0:T(8,128)(2,1)S(1)}, bf16[384,256]{1,0:T(8,128)(2,1)S(1)}, u32[]{:S(2)}, u32[]{:S(2)}) collective-permute-start(bf16[384,256]{1,0:T(8,128)(2,1)S(1)} %fusion.15), channel_id=1, source_target_pairs={{0,32},{32,0},{64,96},{96,64},{128,160},{160,128},{192,224},{224,1... | collective-permute-start | bytes 589832 | tf_op jit(solution)/shard_map/ppermute | solution.py:24
  202.4 5.3 %collective-permute-done.34 = bf16[384,256]{1,0:T(8,128)(2,1)S(1)} collective-permute-done((bf16[384,256]{1,0:T(8,128)(2,1)S(1)}, bf16[384,256]{1,0:T(8,128)(2,1)S(1)}, u32[]{:S(2)}, u32[]{:S(2)}) %collective-permute-start.34) | collective-permute-done | bytes 196640 | tf_op jit(solution)/shard_map/ppermute | solution.py:24
  (170 shorter events, 64.9 us)
Async XLA Ops:
  2.4 16.1 %collective-permute-start = (bf16[384,256]{1,0:T(8,128)(2,1)S(1)}, bf16[384,256]{1,0:T(8,128)(2,1)S(1)}, u32[]{:S(2)}, u32[]{:S(2)}) collective-permute-start(bf16[384,256]{1,0:T(8,128)(2,1)S(1)} %get-tuple-element.21), channel_id=1, source_target_pairs={{0,64},{32,96},{64,0},{96,32},{128,192},{160,224},{192,128},{224,1... | collective-permute-start | bytes 589832 | tf_op jit(solution)/shard_map/ppermute | solution.py:24
  4.1 15.6 %collective-permute-start.2 = (bf16[384,256]{1,0:T(8,128)(2,1)S(1)}, bf16[384,256]{1,0:T(8,128)(2,1)S(1)}, u32[]{:S(2)}, u32[]{:S(2)}) collective-permute-start(bf16[384,256]{1,0:T(8,128)(2,1)S(1)} %get-tuple-element.21), channel_id=1, source_target_pairs={{0,192},{32,224},{64,128},{96,160},{128,64},{160,96},{192,0},{224,... | collective-permute-start | bytes 589832 | tf_op jit(solution)/shard_map/ppermute | solution.py:24
  6.3 13.5 %collective-permute-start.4 = (bf16[384,256]{1,0:T(8,128)(2,1)S(1)}, bf16[384,256]{1,0:T(8,128)(2,1)S(1)}, u32[]{:S(2)}, u32[]{:S(2)}) collective-permute-start(bf16[384,256]{1,0:T(8,128)(2,1)S(1)} %get-tuple-element.21), channel_id=1, source_target_pairs={{0,32},{32,0},{64,96},{96,64},{128,160},{160,128},{192,224},{224,1... | collective-permute-start | bytes 589832 | tf_op jit(solution)/shard_map/ppermute | solution.py:24
  21.8 7.9 %collective-permute-start.7 = (bf16[384,256]{1,0:T(8,128)(2,1)S(1)}, bf16[384,256]{1,0:T(8,128)(2,1)S(1)}, u32[]{:S(2)}, u32[]{:S(2)}) collective-permute-start(bf16[384,256]{1,0:T(8,128)(2,1)S(1)} %collective-permute-done.4), channel_id=1, source_target_pairs={{0,192},{32,224},{64,128},{96,160},{128,64},{160,96},{192,0},{224,... | collective-permute-start | bytes 589832 | tf_op jit(solution)/shard_map/ppermute | solution.py:24
  41.8 8.1 %collective-permute-start.9 = (bf16[24,128,256]{2,1,0:T(8,128)(2,1)S(1)}, bf16[24,128,256]{2,1,0:T(8,128)(2,1)S(1)}, u32[]{:S(2)}, u32[]{:S(2)}) collective-permute-start(bf16[24,128,256]{2,1,0:T(8,128)(2,1)S(1)} %forward2.1), channel_id=1, source_target_pairs={{0,1},{1,0},{2,3},{3,2},{4,5},{5,4},{6,7},{7,6},{8,9},{9,8},{10,11... | collective-permute-start | bytes 4718600 | tf_op jit(solution)/shard_map/ppermute | solution.py:24
  44.5 20.0 %collective-permute-start.14 = (bf16[4,384,256]{2,1,0:T(8,128)(2,1)S(1)}, bf16[4,384,256]{2,1,0:T(8,128)(2,1)S(1)}, u32[]{:S(2)}, u32[]{:S(2)}) collective-permute-start(bf16[4,384,256]{2,1,0:T(8,128)(2,1)S(1)} %bitcast.115), channel_id=1, source_target_pairs={{0,6},{1,7},{2,4},{3,5},{4,2},{5,3},{6,0},{7,1},{8,14},{9,15},{10,... | collective-permute-start | bytes 2359304 | tf_op jit(solution)/shard_map/ppermute | solution.py:24
  44.6 22.0 %collective-permute-start.11 = (bf16[4,384,256]{2,1,0:T(8,128)(2,1)S(1)}, bf16[4,384,256]{2,1,0:T(8,128)(2,1)}, u32[]{:S(2)}, u32[]{:S(2)}) collective-permute-start(bf16[4,384,256]{2,1,0:T(8,128)(2,1)S(1)} %bitcast.114), channel_id=1, source_target_pairs={{0,2},{1,3},{2,0},{3,1},{4,6},{5,7},{6,4},{7,5},{8,10},{9,11},{10,... | collective-permute-start | bytes 2359304 | tf_op jit(solution)/shard_map/ppermute | solution.py:24
  65.5 11.1 %collective-permute-start.15 = (bf16[2,384,256]{2,1,0:T(8,128)(2,1)}, bf16[2,384,256]{2,1,0:T(8,128)(2,1)}, u32[]{:S(2)}, u32[]{:S(2)}) collective-permute-start(bf16[2,384,256]{2,1,0:T(8,128)(2,1)} %fusion.1), channel_id=1, source_target_pairs={{0,2},{1,3},{2,0},{3,1},{4,6},{5,7},{6,4},{7,5},{8,10},{9,11},{10,... | collective-permute-start | bytes 1179656 | tf_op jit(solution)/shard_map/ppermute | solution.py:24
  67.8 12.4 %collective-permute-start.12 = (bf16[2,384,256]{2,1,0:T(8,128)(2,1)S(1)}, bf16[2,384,256]{2,1,0:T(8,128)(2,1)S(1)}, u32[]{:S(2)}, u32[]{:S(2)}) collective-permute-start(bf16[2,384,256]{2,1,0:T(8,128)(2,1)S(1)} %fusion.4), channel_id=1, source_target_pairs={{0,6},{1,7},{2,4},{3,5},{4,2},{5,3},{6,0},{7,1},{8,14},{9,15},{10,... | collective-permute-start | bytes 1179656 | tf_op jit(solution)/shard_map/ppermute | solution.py:24
  77.8 14.6 %collective-permute-start.16 = (bf16[384,256]{1,0:T(8,128)(2,1)S(1)}, bf16[384,256]{1,0:T(8,128)(2,1)S(1)}, u32[]{:S(2)}, u32[]{:S(2)}) collective-permute-start(bf16[384,256]{1,0:T(8,128)(2,1)S(1)} %get-tuple-element.41), channel_id=1, source_target_pairs={{0,16},{1,17},{2,18},{3,19},{4,20},{5,21},{6,22},{7,23},{8,24},{9,... | collective-permute-start | bytes 589832 | tf_op jit(solution)/shard_map/ppermute | solution.py:24
  79.8 12.6 %collective-permute-start.17 = (bf16[384,256]{1,0:T(8,128)(2,1)S(1)}, bf16[384,256]{1,0:T(8,128)(2,1)S(1)}, u32[]{:S(2)}, u32[]{:S(2)}) collective-permute-start(bf16[384,256]{1,0:T(8,128)(2,1)S(1)} %get-tuple-element.42), channel_id=1, source_target_pairs={{0,24},{1,25},{2,26},{3,27},{4,28},{5,29},{6,30},{7,31},{8,16},{9,... | collective-permute-start | bytes 589832 | tf_op jit(solution)/shard_map/ppermute | solution.py:24
  81.4 13.3 %collective-permute-start.13 = (bf16[384,256]{1,0:T(8,128)(2,1)S(1)}, bf16[384,256]{1,0:T(8,128)(2,1)S(1)}, u32[]{:S(2)}, u32[]{:S(2)}) collective-permute-start(bf16[384,256]{1,0:T(8,128)(2,1)S(1)} %fusion.20), channel_id=1, source_target_pairs={{0,8},{1,9},{2,10},{3,11},{4,12},{5,13},{6,14},{7,15},{8,0},{9,1},... | collective-permute-start | bytes 589832 | tf_op jit(solution)/shard_map/ppermute | solution.py:24
  98.2 8.5 %collective-permute-start.37 = (f32[32,256]{1,0:T(8,128)S(1)}, f32[32,256]{1,0:T(8,128)S(1)}, u32[]{:S(2)}, u32[]{:S(2)}) collective-permute-start(f32[32,256]{1,0:T(8,128)S(1)} %get-tuple-element.47), channel_id=1, source_target_pairs={{0,4},{1,5},{2,6},{3,7},{4,0},{5,1},{6,2},{7,3},{8,12},{9,13},{10,... | collective-permute-start | bytes 98312 | tf_op jit(solution)/shard_map/ppermute | solution.py:24
  102.1 10.0 %collective-permute-start.18 = (bf16[384,256]{1,0:T(8,128)(2,1)S(1)}, bf16[384,256]{1,0:T(8,128)(2,1)S(1)}, u32[]{:S(2)}, u32[]{:S(2)}) collective-permute-start(bf16[384,256]{1,0:T(8,128)(2,1)S(1)} %get-tuple-element.55), channel_id=1, source_target_pairs={{0,8},{1,9},{2,10},{3,11},{4,12},{5,13},{6,14},{7,15},{8,0},{9,1},... | collective-permute-start | bytes 589832 | tf_op jit(solution)/shard_map/ppermute | solution.py:24
  104.1 17.2 %collective-permute-start.19 = (bf16[384,256]{1,0:T(8,128)(2,1)S(1)}, bf16[384,256]{1,0:T(8,128)(2,1)S(1)}, u32[]{:S(2)}, u32[]{:S(2)}) collective-permute-start(bf16[384,256]{1,0:T(8,128)(2,1)S(1)} %get-tuple-element.55), channel_id=1, source_target_pairs={{0,16},{1,17},{2,18},{3,19},{4,20},{5,21},{6,22},{7,23},{8,24},{9,... | collective-permute-start | bytes 589832 | tf_op jit(solution)/shard_map/ppermute | solution.py:24
  105.3 16.0 %collective-permute-start.20 = (bf16[384,256]{1,0:T(8,128)(2,1)S(1)}, bf16[384,256]{1,0:T(8,128)(2,1)S(1)}, u32[]{:S(2)}, u32[]{:S(2)}) collective-permute-start(bf16[384,256]{1,0:T(8,128)(2,1)S(1)} %get-tuple-element.55), channel_id=1, source_target_pairs={{0,24},{1,25},{2,26},{3,27},{4,28},{5,29},{6,30},{7,31},{8,16},{9,... | collective-permute-start | bytes 589832 | tf_op jit(solution)/shard_map/ppermute | solution.py:24
  106.7 19.8 %collective-permute-start.39 = (f32[32,256]{1,0:T(8,128)S(1)}, f32[32,256]{1,0:T(8,128)S(1)}, u32[]{:S(2)}, u32[]{:S(2)}) collective-permute-start(f32[32,256]{1,0:T(8,128)S(1)} %add_add_fusion), channel_id=1, source_target_pairs={{0,8},{1,9},{2,10},{3,11},{4,12},{5,13},{6,14},{7,15},{8,0},{9,1},... | collective-permute-start | bytes 98312 | tf_op jit(solution)/shard_map/ppermute | solution.py:24
  121.3 28.1 %collective-permute-start.21 = (bf16[1536,256]{1,0:T(8,128)(2,1)S(1)}, bf16[1536,256]{1,0:T(8,128)(2,1)S(1)}, u32[]{:S(2)}, u32[]{:S(2)}) collective-permute-start(bf16[1536,256]{1,0:T(8,128)(2,1)S(1)} %pad_maximum_fusion), channel_id=1, source_target_pairs={{0,2},{1,3},{2,0},{3,1},{4,6},{5,7},{6,4},{7,5},{8,10},{9,11},{10,... | collective-permute-start | bytes 2359304 | tf_op jit(solution)/shard_map/ppermute | solution.py:24
  124.2 30.2 %collective-permute-start.23 = (bf16[1536,256]{1,0:T(8,128)(2,1)S(1)}, bf16[1536,256]{1,0:T(8,128)(2,1)S(1)}, u32[]{:S(2)}, u32[]{:S(2)}) collective-permute-start(bf16[1536,256]{1,0:T(8,128)(2,1)S(1)} %pad_maximum_fusion), channel_id=1, source_target_pairs={{0,6},{1,7},{2,4},{3,5},{4,2},{5,3},{6,0},{7,1},{8,14},{9,15},{10,... | collective-permute-start | bytes 2359304 | tf_op jit(solution)/shard_map/ppermute | solution.py:24
  132.3 31.8 %collective-permute-start.25 = (bf16[1536,256]{1,0:T(8,128)(2,1)S(1)}, bf16[1536,256]{1,0:T(8,128)(2,1)S(1)}, u32[]{:S(2)}, u32[]{:S(2)}) collective-permute-start(bf16[1536,256]{1,0:T(8,128)(2,1)S(1)} %pad_maximum_fusion), channel_id=1, source_target_pairs={{0,1},{1,0},{2,3},{3,2},{4,5},{5,4},{6,7},{7,6},{8,9},{9,8},{10,11... | collective-permute-start | bytes 2359304 | tf_op jit(solution)/shard_map/ppermute | solution.py:24
  140.9 8.3 %collective-permute-start.43 = (f32[32,256]{1,0:T(8,128)S(1)}, f32[32,256]{1,0:T(8,128)S(1)}, u32[]{:S(2)}, u32[]{:S(2)}) collective-permute-start(f32[32,256]{1,0:T(8,128)S(1)} %add.370), channel_id=1, source_target_pairs={{0,32},{32,0},{64,96},{96,64},{128,160},{160,128},{192,224},{224,1... | collective-permute-start | bytes 98312 | tf_op jit(solution)/shard_map/ppermute | solution.py:24
  149.5 8.4 %collective-permute-start.22 = (bf16[768,256]{1,0:T(8,128)(2,1)S(1)}, bf16[768,256]{1,0:T(8,128)(2,1)S(1)}, u32[]{:S(2)}, u32[]{:S(2)}) collective-permute-start(bf16[768,256]{1,0:T(8,128)(2,1)S(1)} %slice.223), channel_id=1, source_target_pairs={{0,6},{1,7},{2,4},{3,5},{4,2},{5,3},{6,0},{7,1},{8,14},{9,15},{10,... | collective-permute-start | bytes 1179656 | tf_op jit(solution)/shard_map/ppermute | solution.py:24
  152.1 27.2 %collective-permute-start.45 = (f32[32,256]{1,0:T(8,128)S(1)}, f32[32,256]{1,0:T(8,128)S(1)}, u32[]{:S(2)}, u32[]{:S(2)}) collective-permute-start(f32[32,256]{1,0:T(8,128)S(1)} %get-tuple-element.12), channel_id=1, source_target_pairs={{0,4},{1,5},{2,6},{3,7},{4,0},{5,1},{6,2},{7,3},{8,12},{9,13},{10,... | collective-permute-start | bytes 98312 | tf_op jit(solution)/shard_map/ppermute | solution.py:24
  154.5 7.9 %collective-permute-start.24 = (bf16[768,256]{1,0:T(8,128)(2,1)S(1)}, bf16[768,256]{1,0:T(8,128)(2,1)S(1)}, u32[]{:S(2)}, u32[]{:S(2)}) collective-permute-start(bf16[768,256]{1,0:T(8,128)(2,1)S(1)} %slice.224), channel_id=1, source_target_pairs={{0,2},{1,3},{2,0},{3,1},{4,6},{5,7},{6,4},{7,5},{8,10},{9,11},{10,... | collective-permute-start | bytes 1179656 | tf_op jit(solution)/shard_map/ppermute | solution.py:24
  154.7 10.8 %collective-permute-start.26 = (bf16[1536,256]{1,0:T(8,128)(2,1)S(1)}, bf16[1536,256]{1,0:T(8,128)(2,1)S(1)}, u32[]{:S(2)}, u32[]{:S(2)}) collective-permute-start(bf16[1536,256]{1,0:T(8,128)(2,1)S(1)} %collective-permute-done.21), channel_id=1, source_target_pairs={{0,1},{1,0},{2,3},{3,2},{4,5},{5,4},{6,7},{7,6},{8,9},{9,8},{10,11... | collective-permute-start | bytes 2359304 | tf_op jit(solution)/shard_map/ppermute | solution.py:24
  157.9 11.0 %collective-permute-start.29 = (bf16[1536,256]{1,0:T(8,128)(2,1)S(1)}, bf16[1536,256]{1,0:T(8,128)(2,1)S(1)}, u32[]{:S(2)}, u32[]{:S(2)}) collective-permute-start(bf16[1536,256]{1,0:T(8,128)(2,1)S(1)} %collective-permute-done.23), channel_id=1, source_target_pairs={{0,1},{1,0},{2,3},{3,2},{4,5},{5,4},{6,7},{7,6},{8,9},{9,8},{10,11... | collective-permute-start | bytes 2359304 | tf_op jit(solution)/shard_map/ppermute | solution.py:24
  165.5 13.8 %collective-permute-start.46 = (f32[32,256]{1,0:T(8,128)S(1)}, f32[32,256]{1,0:T(8,128)S(1)}, u32[]{:S(2)}, u32[]{:S(2)}) collective-permute-start(f32[32,256]{1,0:T(8,128)S(1)} %get-tuple-element.12), channel_id=1, source_target_pairs={{0,6},{1,7},{2,4},{3,5},{4,2},{5,3},{6,0},{7,1},{8,14},{9,15},{10,... | collective-permute-start | bytes 98312 | tf_op jit(solution)/shard_map/ppermute | solution.py:24
  179.2 11.1 %collective-permute-start.32 = (bf16[2,384,256]{2,1,0:T(8,128)(2,1)S(1)}, bf16[2,384,256]{2,1,0:T(8,128)(2,1)S(1)}, u32[]{:S(2)}, u32[]{:S(2)}) collective-permute-start(bf16[2,384,256]{2,1,0:T(8,128)(2,1)S(1)} %bitcast.117), channel_id=1, source_target_pairs={{0,192},{32,224},{64,128},{96,160},{128,64},{160,96},{192,0},{224,... | collective-permute-start | bytes 1179656 | tf_op jit(solution)/shard_map/ppermute | solution.py:24
  179.3 22.3 %collective-permute-start.47 = (f32[128,256]{1,0:T(8,128)S(1)}, f32[128,256]{1,0:T(8,128)S(1)}, u32[]{:S(2)}, u32[]{:S(2)}) collective-permute-start(f32[128,256]{1,0:T(8,128)S(1)} %constant_dynamic-update-slice_fusion.23), channel_id=1, source_target_pairs={{0,1},{1,0},{2,3},{3,2},{4,5},{5,4},{6,7},{7,6},{8,9},{9,8},{10,11... | collective-permute-start | bytes 393224 | tf_op jit(solution)/shard_map/ppermute | solution.py:24
  179.4 11.6 %collective-permute-start.30 = (bf16[2,384,256]{2,1,0:T(8,128)(2,1)S(1)}, bf16[2,384,256]{2,1,0:T(8,128)(2,1)S(1)}, u32[]{:S(2)}, u32[]{:S(2)}) collective-permute-start(bf16[2,384,256]{2,1,0:T(8,128)(2,1)S(1)} %bitcast.116), channel_id=1, source_target_pairs={{0,64},{32,96},{64,0},{96,32},{128,192},{160,224},{192,128},{224,1... | collective-permute-start | bytes 1179656 | tf_op jit(solution)/shard_map/ppermute | solution.py:24
  191.1 11.2 %collective-permute-start.31 = (bf16[384,256]{1,0:T(8,128)(2,1)S(1)}, bf16[384,256]{1,0:T(8,128)(2,1)S(1)}, u32[]{:S(2)}, u32[]{:S(2)}) collective-permute-start(bf16[384,256]{1,0:T(8,128)(2,1)S(1)} %fusion.16), channel_id=1, source_target_pairs={{0,192},{32,224},{64,128},{96,160},{128,64},{160,96},{192,0},{224,... | collective-permute-start | bytes 589832 | tf_op jit(solution)/shard_map/ppermute | solution.py:24
  196.2 11.5 %collective-permute-start.34 = (bf16[384,256]{1,0:T(8,128)(2,1)S(1)}, bf16[384,256]{1,0:T(8,128)(2,1)S(1)}, u32[]{:S(2)}, u32[]{:S(2)}) collective-permute-start(bf16[384,256]{1,0:T(8,128)(2,1)S(1)} %fusion.15), channel_id=1, source_target_pairs={{0,32},{32,0},{64,96},{96,64},{128,160},{160,128},{192,224},{224,1... | collective-permute-start | bytes 589832 | tf_op jit(solution)/shard_map/ppermute | solution.py:24
  (26 other events, 270.3 us)
